TPU v7x, 32 devices: a whole 2x2x4 slice. The times are simulated.
32 devices in a mesh: gx: 2 (over y), gy: 4 (over x, core), shot: 4 (over z).
Axes of the slice: x: 2, y: 2, z: 4, core: 2. Of those that a mesh axis runs over, the one named last changes fastest.
Arguments:
- adj_prev: float32 [4, 64, 64, 256], P('shot', 'gx', 'gy'), may hold values from -6 to 6
- adj_cur: float32 [4, 64, 64, 256], P('shot', 'gx', 'gy'), may hold values from -6 to 6
- fwd_accel: bfloat16 [4, 4, 64, 64, 256], P('shot', None, 'gx', 'gy'), may hold values from -6 to 6
- courant2: float32 [64, 64, 256], P('gx', 'gy'), may hold values from 0.05 to 0.18
- traces: bfloat16 [4, 4, 512], P('shot', None, ('gx', 'gy')), may hold values from -6 to 6
- weights: bfloat16 [2, 4, 64, 16, 256], P('gx', 'gy'), may hold values from -3 to 3
- rblock: int32 [2, 4, 64], P('gx', 'gy'), may hold values from 0 to 31
- column: int32 [2, 4, 64], P('gx', 'gy'), may hold values from 0 to 511
- counts: int32 [2, 4], P('gx', 'gy'), may hold values from 16 to 64
Outputs:
- adj_prev_out: float32 [4, 64, 64, 256], P('shot', 'gx', 'gy')
- adj_cur_out: float32 [4, 64, 64, 256], P('shot', 'gx', 'gy')
- gradient: float32 [32, 32, 128], P('gx', 'gy')
All inputs are finite; a program needn't handle non-finite values.
Results may differ from a plain program's by a relative error of at most 0.00045.
Values may be sent and summed in bfloat16 or wider, within the bound.
No kernel may reach another device: no remote copies, remote signals or barrier semaphores. Data moves between devices by JAX's collectives and lax.ppermute only.
A program may use at most 128 MiB of HBM per device.

v0:
```python
import jax
import jax.numpy as jnp
from jax import lax
from jax.sharding import PartitionSpec as P

LAPLACE_COEFS = (-205.0 / 72.0, 8.0 / 5.0, -1.0 / 5.0, 8.0 / 315.0, -1.0 / 560.0)


def padded_2(block, sides, width):
    for axis, dim in sides:
        count = lax.axis_size(axis)
        forward = [(i, i + 1) for i in range(count - 1)]
        backward = [(target, source) for source, target in forward]
        low = lax.ppermute(
            lax.slice_in_dim(block, block.shape[dim] - width, None, axis=dim), axis, forward
        )
        high = lax.ppermute(lax.slice_in_dim(block, 0, width, axis=dim), axis, backward)
        block = jnp.concatenate([low, block, high], axis=dim)
    return block


def laplace_padded(padded_xy, size_x, size_y, size_z):
    padded = jnp.pad(padded_xy, ((0, 0), (0, 0), (4, 4)))
    center = padded[4 : 4 + size_x, 4 : 4 + size_y, 4 : 4 + size_z]
    total = 3.0 * LAPLACE_COEFS[0] * center
    for offset in range(1, 5):
        weight = LAPLACE_COEFS[offset]
        total = total + weight * (
            padded[4 + offset : 4 + offset + size_x, 4 : 4 + size_y, 4 : 4 + size_z]
            + padded[4 - offset : 4 - offset + size_x, 4 : 4 + size_y, 4 : 4 + size_z]
        )
        total = total + weight * (
            padded[4 : 4 + size_x, 4 + offset : 4 + offset + size_y, 4 : 4 + size_z]
            + padded[4 : 4 + size_x, 4 - offset : 4 - offset + size_y, 4 : 4 + size_z]
        )
        total = total + weight * (
            padded[4 : 4 + size_x, 4 : 4 + size_y, 4 + offset : 4 + offset + size_z]
            + padded[4 : 4 + size_x, 4 : 4 + size_y, 4 - offset : 4 - offset + size_z]
        )
    return total


def extend(field):
    return padded_2(field, (("gx", 0), ("gy", 1)), 4)


def restrict(fine):
    size_x, size_y, size_z = fine.shape
    return fine.reshape(size_x // 2, 2, size_y // 2, 2, size_z // 2, 2).mean(axis=(1, 3, 5))


def local(adj_prev, adj_cur, fwd_accel, courant2, traces, weights, rblock, column, counts):
    previous = adj_prev[0]
    current = adj_cur[0]
    size_x, size_y, size_z = current.shape
    steps = fwd_accel.shape[1]
    slots = weights.shape[2]
    recv_block = weights.shape[3]
    gathered = lax.all_gather(traces, ("gx", "gy"), axis=2, tiled=True)
    blocks = gathered[0].reshape(steps, -1, recv_block)
    picked = jnp.take(blocks, rblock[0, 0], axis=1)
    contrib = jnp.einsum("tsr,srz->tsz", picked, weights[0, 0], preferred_element_type=jnp.float32)
    live_slots = (jnp.arange(slots, dtype=jnp.int32) < counts[0, 0]).astype(jnp.float32)
    onehot = (
        column[0, 0][:, None] == jnp.arange(size_x * size_y, dtype=jnp.int32)[None, :]
    ).astype(jnp.float32) * live_slots[:, None]
    source = jnp.einsum("sc,tsz->tcz", onehot, contrib, precision=lax.Precision.HIGHEST).reshape(
        steps, size_x, size_y, size_z
    )
    fine = jnp.zeros(current.shape, jnp.float32)
    for step_index in range(steps):
        padded_xy = extend(current)
        next_field = (
            2.0 * current
            - previous
            + courant2 * laplace_padded(padded_xy, size_x, size_y, size_z)
            + source[step_index]
        )
        fine = fine + fwd_accel[0, step_index].astype(jnp.float32) * next_field
        previous, current = (current, next_field)
    gradient = lax.psum(restrict(fine), "shot")
    return (previous[None], current[None], gradient)


def solution(mesh):
    return jax.shard_map(
        local,
        mesh=mesh,
        in_specs=(
            P("shot", "gx", "gy", None),
            P("shot", "gx", "gy", None),
            P("shot", None, "gx", "gy", None),
            P("gx", "gy", None),
            P("shot", None, ("gx", "gy")),
            P("gx", "gy", None, None, None),
            P("gx", "gy", None),
            P("gx", "gy", None),
            P("gx", "gy"),
        ),
        out_specs=(P("shot", "gx", "gy", None), P("shot", "gx", "gy", None), P("gx", "gy", None)),
        check_vma=False,
    )
```

profile of v0, /device:TPU:0, one launch (start us, length us, event | category | flops | bytes accessed | tf_op | source)
XLA Modules:
  0.0 203.9 jit_solution(15450160707005926613)
XLA Ops:
  7.2 0.9 slice_bitcast_fusion.1
  8.2 1.3 collective-permute-start
  9.5 4.9 %collective-permute-start.1 = (f32[4,16,256]{2,1,0:T(8,128)S(1)}, f32[4,16,256]{2,1,0:T(8,128)S(1)}, u32[]{:S(2)}, u32[]{:S(2)}) collective-permute-start(f32[4,16,256]{2,1,0:T(8,128)S(1)} %get-tuple-element.32), channel_id=1, source_target_pairs={{0,16},{1,17},{2,18},{3,19},{4,20},{5,21},{6,22},{7,23},{8,24},{9,... | collective-permute-start | bytes 196616 | tf_op jit(solution)/shard_map/ppermute | solution.py:14
  15.0 0.7 compare_and_fusion
  16.4 0.8 copy.21
  17.2 10.4 %all_gather.3 = bf16[1,4,512]{1,0,2:T(2,128)(2,1)S(1)} all-gather(bf16[1,4,64]{1,0,2:T(2,128)(2,1)S(1)} %copy.21), channel_id=1, replica_groups=mesh['gx'=2,'gy'=4,'shot'=4] {'gx','gy'}, dimensions={2}, use_global_device_ids=true | all-gather | bytes 4608 | tf_op jit(solution)/shard_map/all_gather | solution.py:59
  28.8 1.9 convolution_bitcast_fusion
  30.8 2.3 %collective-permute-start.3 = (f32[40,4,256]{2,1,0:T(4,128)S(1)}, f32[40,4,256]{2,1,0:T(4,128)S(1)}, u32[]{:S(2)}, u32[]{:S(2)}) collective-permute-start(f32[40,4,256]{2,1,0:T(4,128)S(1)} %get-tuple-element.23), channel_id=1, source_target_pairs={{0,4},{4,8},{8,12},{1,5},{5,9},{9,13},{2,6},{6,10},{10,14},{3,7},{... | collective-permute-start | bytes 491528 | tf_op jit(solution)/shard_map/ppermute | solution.py:14
  33.0 1.3 collective-permute-start.2
  34.3 1.2 fusion.167
  36.3 0.8 select_maximum_fusion.12
  37.3 0.9 copy-done.3
  38.3 2.0 fusion.93
  40.3 1.4 collective-permute-start.4
  41.8 4.5 %collective-permute-start.5 = (f32[4,16,256]{2,1,0:T(8,128)S(1)}, f32[4,16,256]{2,1,0:T(8,128)S(1)}, u32[]{:S(2)}, u32[]{:S(2)}) collective-permute-start(f32[4,16,256]{2,1,0:T(8,128)S(1)} %get-tuple-element.30), channel_id=1, source_target_pairs={{0,16},{1,17},{2,18},{3,19},{4,20},{5,21},{6,22},{7,23},{8,24},{9,... | collective-permute-start | bytes 196616 | tf_op jit(solution)/shard_map/ppermute | solution.py:14
  46.6 1.6 collective-permute-done.5
  48.2 0.8 pad_maximum_fusion.18
  49.0 4.1 %collective-permute-start.7 = (f32[40,4,256]{2,1,0:T(4,128)}, f32[40,4,256]{2,1,0:T(4,128)S(1)}, u32[]{:S(2)}, u32[]{:S(2)}) collective-permute-start(f32[40,4,256]{2,1,0:T(4,128)} %get-tuple-element.19), channel_id=1, source_target_pairs={{0,4},{4,8},{8,12},{1,5},{5,9},{9,13},{2,6},{6,10},{10,14},{3,7},{... | collective-permute-start | bytes 491528 | tf_op jit(solution)/shard_map/ppermute | solution.py:14
  53.1 1.3 collective-permute-start.6
  54.7 2.6 %collective-permute-done.6 = f32[40,4,256]{2,1,0:T(4,128)} collective-permute-done((f32[40,4,256]{2,1,0:T(4,128)}, f32[40,4,256]{2,1,0:T(4,128)}, u32[]{:S(2)}, u32[]{:S(2)}) %collective-permute-start.6) | collective-permute-done | bytes 163872 | tf_op jit(solution)/shard_map/ppermute | solution.py:17
  57.2 1.7 select_maximum_fusion.8
  58.9 1.1 pad_maximum_fusion.1
  60.0 2.0 fusion.66
  62.1 1.4 collective-permute-start.8
  63.5 4.5 %collective-permute-start.9 = (f32[4,16,256]{2,1,0:T(8,128)S(1)}, f32[4,16,256]{2,1,0:T(8,128)S(1)}, u32[]{:S(2)}, u32[]{:S(2)}) collective-permute-start(f32[4,16,256]{2,1,0:T(8,128)S(1)} %get-tuple-element.28), channel_id=1, source_target_pairs={{0,16},{1,17},{2,18},{3,19},{4,20},{5,21},{6,22},{7,23},{8,24},{9,... | collective-permute-start | bytes 196616 | tf_op jit(solution)/shard_map/ppermute | solution.py:14
  68.3 1.6 collective-permute-done.9
  69.9 0.8 pad_maximum_fusion.15
  70.7 4.6 %collective-permute-start.11 = (f32[40,4,256]{2,1,0:T(4,128)}, f32[40,4,256]{2,1,0:T(4,128)S(1)}, u32[]{:S(2)}, u32[]{:S(2)}) collective-permute-start(f32[40,4,256]{2,1,0:T(4,128)} %get-tuple-element.15), channel_id=1, source_target_pairs={{0,4},{4,8},{8,12},{1,5},{5,9},{9,13},{2,6},{6,10},{10,14},{3,7},{... | collective-permute-start | bytes 491528 | tf_op jit(solution)/shard_map/ppermute | solution.py:14
  75.3 1.3 collective-permute-start.10
  76.8 2.6 %collective-permute-done.10 = f32[40,4,256]{2,1,0:T(4,128)} collective-permute-done((f32[40,4,256]{2,1,0:T(4,128)}, f32[40,4,256]{2,1,0:T(4,128)}, u32[]{:S(2)}, u32[]{:S(2)}) %collective-permute-start.10) | collective-permute-done | bytes 163872 | tf_op jit(solution)/shard_map/ppermute | solution.py:17
  79.4 1.7 select_maximum_fusion.4
  81.1 1.1 pad_maximum_fusion.2
  82.2 2.0 fusion.39
  84.2 4.4 %collective-permute-start.13 = (f32[4,16,256]{2,1,0:T(8,128)S(1)}, f32[4,16,256]{2,1,0:T(8,128)S(1)}, u32[]{:S(2)}, u32[]{:S(2)}) collective-permute-start(f32[4,16,256]{2,1,0:T(8,128)S(1)} %get-tuple-element.25), channel_id=1, source_target_pairs={{0,16},{1,17},{2,18},{3,19},{4,20},{5,21},{6,22},{7,23},{8,24},{9,... | collective-permute-start | bytes 196616 | tf_op jit(solution)/shard_map/ppermute | solution.py:14
  88.6 1.3 collective-permute-start.12
  90.5 4.3 %collective-permute-done.12 = f32[4,16,256]{2,1,0:T(8,128)S(1)} collective-permute-done((f32[4,16,256]{2,1,0:T(8,128)S(1)}, f32[4,16,256]{2,1,0:T(8,128)S(1)}, u32[]{:S(2)}, u32[]{:S(2)}) %collective-permute-start.12) | collective-permute-done | bytes 65568 | tf_op jit(solution)/shard_map/ppermute | solution.py:17
  94.8 0.8 pad_maximum_fusion.12
  95.6 4.3 %collective-permute-start.15 = (f32[40,4,256]{2,1,0:T(4,128)}, f32[40,4,256]{2,1,0:T(4,128)S(1)}, u32[]{:S(2)}, u32[]{:S(2)}) collective-permute-start(f32[40,4,256]{2,1,0:T(4,128)} %get-tuple-element.11), channel_id=1, source_target_pairs={{0,4},{4,8},{8,12},{1,5},{5,9},{9,13},{2,6},{6,10},{10,14},{3,7},{... | collective-permute-start | bytes 491528 | tf_op jit(solution)/shard_map/ppermute | solution.py:14
  99.9 1.5 collective-permute-start.14
  101.4 1.0 copy.28
  102.4 1.9 collective-permute-done.14
  104.3 1.7 select_maximum_fusion
  106.0 1.2 pad_maximum_fusion.3
  107.4 2.9 %fusion.149 = (f32[32,16,256]{2,1,0:T(8,128)S(1)}, f32[32,16,256]{2,1,0:T(8,128)}) fusion(f32[32,16,256]{2,1,0:T(8,128)S(1)} %fusion.39, f32[32,16,256]{2,1,0:T(8,128)S(1)} %fusion.66, f32[32,16,256]{2,1,0:T(8,128)S(1)} %fusion.93, bf16[1,4,32,16,256]{4,3,2,1,0:T(8,128)(2,1)S(1)} %copy-done.8, f32[32,16,256]{2,1,0:T(8,128)S(1)} %bitcast.55, ...), kind=kLoop, calls=%fused_computation.267 | loop fusion | flops 7995392 | bytes 13238272 | tf_op jit(solution)/shard_map/add | solution.py:79
  110.3 34.8 %reshape.68 = f32[16,2,8,2,128,2]{5,4,3,2,1,0:T(8,128)} reshape(f32[32,16,256]{2,1,0:T(8,128)S(1)} %get-tuple-element.3) | data formatting | bytes 1048576 | tf_op jit(solution)/shard_map/reshape | solution.py:49
  145.1 12.2 %reduce_sum.9 = f32[16,8,128]{2,1,0:T(8,128)S(1)} reduce(f32[16,2,8,2,128,2]{5,4,3,2,1,0:T(8,128)} %reshape.68, f32[]{:T(128)} %constant.9.clone.1), dimensions={1,3,5}, to_apply=%region_0.1 | reduce | flops 114688 | bytes 589828 | tf_op jit(solution)/shard_map/reduce_sum | solution.py:49
  158.0 37.6 %all-reduce.6.cloned.1.call-done = f32[16,8,128]{2,1,0:T(8,128)} async-done(((f32[16,8,128]{2,1,0:T(8,128)}), f32[16,8,128]{2,1,0:T(8,128)}) %all-reduce.6.cloned.1.call-update) | async-done | bytes 65552 | tf_op jit(solution)/shard_map/psum | solution.py:81
  195.6 1.5 copy.33
  (50 shorter events, 5.6 us)
Async XLA Ops:
  7.2 21.3 %copy-start = (bf16[1,1,64,16,256]{4,3,2,1,0:T(8,128)(2,1)S(1)}, bf16[1,1,64,16,256]{4,3,2,1,0:T(8,128)(2,1)}, u32[]{:S(2)}) copy-start(bf16[1,1,64,16,256]{4,3,2,1,0:T(8,128)(2,1)} %param.14) | copy-start | bytes 1572868
  7.2 21.6 %copy-start.10 = (s32[1,1,64]{2,1,0:T(1,128)S(1)}, s32[1,1,64]{2,1,0:T(1,128)}, u32[]{:S(2)}) copy-start(s32[1,1,64]{2,1,0:T(1,128)} %param.16) | copy-start | bytes 772
  7.2 188.4 %all-reduce.6.cloned.1.call-start = ((), (), s32[]{:S(2)}) async-start(), calls=%async_computation | async-start | bytes 131072 | tf_op jit(solution)/shard_map/psum | solution.py:81
  8.2 22.5 %collective-permute-start = (f32[4,16,256]{2,1,0:T(8,128)S(1)}, f32[4,16,256]{2,1,0:T(8,128)S(1)}, u32[]{:S(2)}, u32[]{:S(2)}) collective-permute-start(f32[4,16,256]{2,1,0:T(8,128)S(1)} %get-tuple-element.31), channel_id=1, source_target_pairs={{16,0},{17,1},{18,2},{19,3},{20,4},{21,5},{22,6},{23,7},{24,8},{25... | collective-permute-start | bytes 196616 | tf_op jit(solution)/shard_map/ppermute | solution.py:17
  9.5 21.2 %collective-permute-start.1 = (f32[4,16,256]{2,1,0:T(8,128)S(1)}, f32[4,16,256]{2,1,0:T(8,128)S(1)}, u32[]{:S(2)}, u32[]{:S(2)}) collective-permute-start(f32[4,16,256]{2,1,0:T(8,128)S(1)} %get-tuple-element.32), channel_id=1, source_target_pairs={{0,16},{1,17},{2,18},{3,19},{4,20},{5,21},{6,22},{7,23},{8,24},{9,... | collective-permute-start | bytes 196616 | tf_op jit(solution)/shard_map/ppermute | solution.py:14
  28.5 2.2 %copy-start.1 = (f32[1,32,16,256]{3,2,1,0:T(8,128)S(1)}, f32[1,32,16,256]{3,2,1,0:T(8,128)}, u32[]{:S(2)}) copy-start(f32[1,32,16,256]{3,2,1,0:T(8,128)} %param.10) | copy-start | bytes 1572868
  30.8 5.0 %collective-permute-start.3 = (f32[40,4,256]{2,1,0:T(4,128)S(1)}, f32[40,4,256]{2,1,0:T(4,128)S(1)}, u32[]{:S(2)}, u32[]{:S(2)}) collective-permute-start(f32[40,4,256]{2,1,0:T(4,128)S(1)} %get-tuple-element.23), channel_id=1, source_target_pairs={{0,4},{4,8},{8,12},{1,5},{5,9},{9,13},{2,6},{6,10},{10,14},{3,7},{... | collective-permute-start | bytes 491528 | tf_op jit(solution)/shard_map/ppermute | solution.py:14
  33.0 3.3 %collective-permute-start.2 = (f32[40,4,256]{2,1,0:T(4,128)S(1)}, f32[40,4,256]{2,1,0:T(4,128)S(1)}, u32[]{:S(2)}, u32[]{:S(2)}) collective-permute-start(f32[40,4,256]{2,1,0:T(4,128)S(1)} %get-tuple-element.24), channel_id=1, source_target_pairs={{4,0},{8,4},{12,8},{5,1},{9,5},{13,9},{6,2},{10,6},{14,10},{7,3},{... | collective-permute-start | bytes 491528 | tf_op jit(solution)/shard_map/ppermute | solution.py:17
  37.1 1.0 copy-start.3
  37.1 1.2 copy-start.9
  40.3 14.1 %copy-start.7 = (f32[1,512,256]{1,2,0:T(8,128)S(1)}, f32[1,512,256]{1,2,0:T(8,128)}, u32[]{:S(2)}) copy-start(f32[1,512,256]{1,2,0:T(8,128)} %get-tuple-element.7) | copy-start | bytes 1572868
  40.3 6.3 %collective-permute-start.4 = (f32[4,16,256]{2,1,0:T(8,128)S(1)}, f32[4,16,256]{2,1,0:T(8,128)S(1)}, u32[]{:S(2)}, u32[]{:S(2)}) collective-permute-start(f32[4,16,256]{2,1,0:T(8,128)S(1)} %get-tuple-element.29), channel_id=1, source_target_pairs={{16,0},{17,1},{18,2},{19,3},{20,4},{21,5},{22,6},{23,7},{24,8},{25... | collective-permute-start | bytes 196616 | tf_op jit(solution)/shard_map/ppermute | solution.py:17
  41.8 6.4 %collective-permute-start.5 = (f32[4,16,256]{2,1,0:T(8,128)S(1)}, f32[4,16,256]{2,1,0:T(8,128)S(1)}, u32[]{:S(2)}, u32[]{:S(2)}) collective-permute-start(f32[4,16,256]{2,1,0:T(8,128)S(1)} %get-tuple-element.30), channel_id=1, source_target_pairs={{0,16},{1,17},{2,18},{3,19},{4,20},{5,21},{6,22},{7,23},{8,24},{9,... | collective-permute-start | bytes 196616 | tf_op jit(solution)/shard_map/ppermute | solution.py:14
  49.0 5.6 %collective-permute-start.7 = (f32[40,4,256]{2,1,0:T(4,128)}, f32[40,4,256]{2,1,0:T(4,128)S(1)}, u32[]{:S(2)}, u32[]{:S(2)}) collective-permute-start(f32[40,4,256]{2,1,0:T(4,128)} %get-tuple-element.19), channel_id=1, source_target_pairs={{0,4},{4,8},{8,12},{1,5},{5,9},{9,13},{2,6},{6,10},{10,14},{3,7},{... | collective-permute-start | bytes 491528 | tf_op jit(solution)/shard_map/ppermute | solution.py:14
  53.1 4.1 %collective-permute-start.6 = (f32[40,4,256]{2,1,0:T(4,128)}, f32[40,4,256]{2,1,0:T(4,128)}, u32[]{:S(2)}, u32[]{:S(2)}) collective-permute-start(f32[40,4,256]{2,1,0:T(4,128)} %get-tuple-element.20), channel_id=1, source_target_pairs={{4,0},{8,4},{12,8},{5,1},{9,5},{13,9},{6,2},{10,6},{14,10},{7,3},{... | collective-permute-start | bytes 491528 | tf_op jit(solution)/shard_map/ppermute | solution.py:17
  62.0 14.6 %copy-start.6 = (f32[1,512,256]{1,2,0:T(8,128)S(1)}, f32[1,512,256]{1,2,0:T(8,128)}, u32[]{:S(2)}) copy-start(f32[1,512,256]{1,2,0:T(8,128)} %get-tuple-element.6) | copy-start | bytes 1572868
  62.1 6.3 %collective-permute-start.8 = (f32[4,16,256]{2,1,0:T(8,128)S(1)}, f32[4,16,256]{2,1,0:T(8,128)S(1)}, u32[]{:S(2)}, u32[]{:S(2)}) collective-permute-start(f32[4,16,256]{2,1,0:T(8,128)S(1)} %get-tuple-element.27), channel_id=1, source_target_pairs={{16,0},{17,1},{18,2},{19,3},{20,4},{21,5},{22,6},{23,7},{24,8},{25... | collective-permute-start | bytes 196616 | tf_op jit(solution)/shard_map/ppermute | solution.py:17
  63.5 6.4 %collective-permute-start.9 = (f32[4,16,256]{2,1,0:T(8,128)S(1)}, f32[4,16,256]{2,1,0:T(8,128)S(1)}, u32[]{:S(2)}, u32[]{:S(2)}) collective-permute-start(f32[4,16,256]{2,1,0:T(8,128)S(1)} %get-tuple-element.28), channel_id=1, source_target_pairs={{0,16},{1,17},{2,18},{3,19},{4,20},{5,21},{6,22},{7,23},{8,24},{9,... | collective-permute-start | bytes 196616 | tf_op jit(solution)/shard_map/ppermute | solution.py:14
  70.7 6.1 %collective-permute-start.11 = (f32[40,4,256]{2,1,0:T(4,128)}, f32[40,4,256]{2,1,0:T(4,128)S(1)}, u32[]{:S(2)}, u32[]{:S(2)}) collective-permute-start(f32[40,4,256]{2,1,0:T(4,128)} %get-tuple-element.15), channel_id=1, source_target_pairs={{0,4},{4,8},{8,12},{1,5},{5,9},{9,13},{2,6},{6,10},{10,14},{3,7},{... | collective-permute-start | bytes 491528 | tf_op jit(solution)/shard_map/ppermute | solution.py:14
  75.3 4.1 %collective-permute-start.10 = (f32[40,4,256]{2,1,0:T(4,128)}, f32[40,4,256]{2,1,0:T(4,128)}, u32[]{:S(2)}, u32[]{:S(2)}) collective-permute-start(f32[40,4,256]{2,1,0:T(4,128)} %get-tuple-element.16), channel_id=1, source_target_pairs={{4,0},{8,4},{12,8},{5,1},{9,5},{13,9},{6,2},{10,6},{14,10},{7,3},{... | collective-permute-start | bytes 491528 | tf_op jit(solution)/shard_map/ppermute | solution.py:17
  84.2 23.0 %copy-start.2 = (f32[32,16,256]{2,1,0:T(8,128)}, f32[32,16,256]{2,1,0:T(8,128)S(1)}, u32[]{:S(2)}) copy-start(f32[32,16,256]{2,1,0:T(8,128)S(1)} %fusion.39) | copy-start | bytes 1572868
  84.2 17.2 %copy-start.5 = (f32[1,512,256]{1,2,0:T(8,128)S(1)}, f32[1,512,256]{1,2,0:T(8,128)}, u32[]{:S(2)}) copy-start(f32[1,512,256]{1,2,0:T(8,128)} %get-tuple-element.5) | copy-start | bytes 1572868
  84.2 6.3 %collective-permute-start.13 = (f32[4,16,256]{2,1,0:T(8,128)S(1)}, f32[4,16,256]{2,1,0:T(8,128)S(1)}, u32[]{:S(2)}, u32[]{:S(2)}) collective-permute-start(f32[4,16,256]{2,1,0:T(8,128)S(1)} %get-tuple-element.25), channel_id=1, source_target_pairs={{0,16},{1,17},{2,18},{3,19},{4,20},{5,21},{6,22},{7,23},{8,24},{9,... | collective-permute-start | bytes 196616 | tf_op jit(solution)/shard_map/ppermute | solution.py:14
  88.6 6.2 %collective-permute-start.12 = (f32[4,16,256]{2,1,0:T(8,128)S(1)}, f32[4,16,256]{2,1,0:T(8,128)S(1)}, u32[]{:S(2)}, u32[]{:S(2)}) collective-permute-start(f32[4,16,256]{2,1,0:T(8,128)S(1)} %get-tuple-element.26), channel_id=1, source_target_pairs={{16,0},{17,1},{18,2},{19,3},{20,4},{21,5},{22,6},{23,7},{24,8},{25... | collective-permute-start | bytes 196616 | tf_op jit(solution)/shard_map/ppermute | solution.py:17
  95.6 6.8 %collective-permute-start.15 = (f32[40,4,256]{2,1,0:T(4,128)}, f32[40,4,256]{2,1,0:T(4,128)S(1)}, u32[]{:S(2)}, u32[]{:S(2)}) collective-permute-start(f32[40,4,256]{2,1,0:T(4,128)} %get-tuple-element.11), channel_id=1, source_target_pairs={{0,4},{4,8},{8,12},{1,5},{5,9},{9,13},{2,6},{6,10},{10,14},{3,7},{... | collective-permute-start | bytes 491528 | tf_op jit(solution)/shard_map/ppermute | solution.py:14
  99.9 4.4 %collective-permute-start.14 = (f32[40,4,256]{2,1,0:T(4,128)}, f32[40,4,256]{2,1,0:T(4,128)}, u32[]{:S(2)}, u32[]{:S(2)}) collective-permute-start(f32[40,4,256]{2,1,0:T(4,128)} %get-tuple-element.12), channel_id=1, source_target_pairs={{4,0},{8,4},{12,8},{5,1},{9,5},{13,9},{6,2},{10,6},{14,10},{7,3},{... | collective-permute-start | bytes 491528 | tf_op jit(solution)/shard_map/ppermute | solution.py:17
  106.0 1.2 copy-start.4
  106.0 1.5 copy-start.8
Sparse Core Ops, SparseCore 0:
  158.1 37.4 all-reduce.5
where the time goes:
time: 205 us; the launch traced here: 204 us
  waiting for transfers between devices  53.9 us (26%)
  starting transfers between devices  44.5 us (22%)
  local copies, waits for them, and re-layouts  43 us (21%)
  other arithmetic  34.7 us (17%)
  between operations  15.2 us (7%)
  blocking collectives  10.4 us (5%)
  matrix products  2.15 us (1%)
    psum x1, waiting for transfers between devices, local(): gradient = lax.psum(restrict(fine), 'shot')  37.6 us
    reshape x1, local copies, waits for them, and re-layouts, restrict(): fine.reshape(size_x // 2, 2, size_y // 2, 2, size_z // 2, 2)  34.8 us
    ppermute x8, starting transfers between devices, padded_2(): lax.ppermute(lax.slice_in_dim(block, block.shape[dim] - width, None, axis...  33.7 us
    ppermute x8, waiting for transfers between devices, padded_2(): lax.ppermute(lax.slice_in_dim(block, 0, width, axis=dim), axis, backward)  12.5 us
    reduce_sum x1, other arithmetic, restrict(): fine.reshape(size_x // 2, 2, size_y // 2, 2, size_z // 2, 2)  12.2 us
    concatenate x12, other arithmetic, padded_2(): block = jnp.concatenate([low, block, high], axis=dim)  11.7 us
    ppermute x8, starting transfers between devices, padded_2(): lax.ppermute(lax.slice_in_dim(block, 0, width, axis=dim), axis, backward)  10.8 us
    all_gather x1, blocking collectives, local(): gathered = lax.all_gather(traces, ('gx', 'gy'), axis=2, tiled=True)  10.4 us
  transfers between devices with their start and end apart: 17, of which 11 were waited for; matrix products, arithmetic and copies ran while one was open for 4% of the time, Pallas kernels for 0%

commit v1 on v0

--- a/solution.py
+++ b/solution.py
@@ -2,6 +2,7 @@
 import jax.numpy as jnp
 from jax import lax
 from jax.sharding import PartitionSpec as P
+from jax.lax import all_gather
 
 LAPLACE_COEFS = (-205.0 / 72.0, 8.0 / 5.0, -1.0 / 5.0, 8.0 / 315.0, -1.0 / 560.0)
 
@@ -78,7 +79,8 @@
         )
         fine = fine + fwd_accel[0, step_index].astype(jnp.float32) * next_field
         previous, current = (current, next_field)
-    gradient = lax.psum(restrict(fine), "shot")
+    payload = restrict(fine)
+    gradient = all_gather(payload, axis_name="shot").sum(axis=0)
     return (previous[None], current[None], gradient)
 
 

time: 205 us -> 168 us (0.82)
  waiting for transfers between devices: 53.9 us -> 16.3 us
  blocking collectives: 10.4 us -> 25.2 us
  between operations: 15.2 us -> 1.8 us
    psum x1 -> x0, waiting for transfers between devices: 37.6 us -> none  [local(): gradient = lax.psum(restrict(fine), 'shot')]
    all_gather x0 -> x1, blocking collectives: none -> 14.8 us  [local(): gradient = all_gather(payload, axis_name='shot').sum(axis=0)]
  transfers between devices with their start and end apart: 17 -> 16, of which waited for: 11 -> 10; matrix products, arithmetic and copies ran while one was open for 4% -> 5% of each run, Pallas kernels for 0% -> 0%
where the time goes in v1:
time: 168 us; the launch traced here: 166 us
  starting transfers between devices  44.4 us (26%)
  local copies, waits for them, and re-layouts  41.6 us (25%)
  other arithmetic  34.8 us (21%)
  blocking collectives  25.2 us (15%)
  waiting for transfers between devices  16.3 us (10%)
  matrix products  2.15 us (1%)
  between operations  1.8 us (1%)
    reshape x1, local copies, waits for them, and re-layouts, restrict(): fine.reshape(size_x // 2, 2, size_y // 2, 2, size_z // 2, 2)  34.8 us
    ppermute x8, starting transfers between devices, padded_2(): lax.ppermute(lax.slice_in_dim(block, block.shape[dim] - width, None, axis...  33.7 us
    all_gather x1, blocking collectives, local(): gradient = all_gather(payload, axis_name='shot').sum(axis=0)  14.8 us
    ppermute x8, waiting for transfers between devices, padded_2(): lax.ppermute(lax.slice_in_dim(block, 0, width, axis=dim), axis, backward)  12.6 us
    reduce_sum x1, other arithmetic, restrict(): fine.reshape(size_x // 2, 2, size_y // 2, 2, size_z // 2, 2)  12.2 us
    concatenate x12, other arithmetic, padded_2(): block = jnp.concatenate([low, block, high], axis=dim)  11.7 us
    ppermute x8, starting transfers between devices, padded_2(): lax.ppermute(lax.slice_in_dim(block, 0, width, axis=dim), axis, backward)  10.8 us
    all_gather x1, blocking collectives, local(): gathered = lax.all_gather(traces, ('gx', 'gy'), axis=2, tiled=True)  10.4 us
  transfers between devices with their start and end apart: 16, of which 10 were waited for; matrix products, arithmetic and copies ran while one was open for 5% of the time, Pallas kernels for 0%

profile of v1, /device:TPU:0, one launch (start us, length us, event | category | flops | bytes accessed | tf_op | source)
XLA Modules:
  0.0 166.3 jit_solution(9032730978474133348)
XLA Ops:
  0.7 0.9 slice_bitcast_fusion.1
  1.6 1.3 collective-permute-start
  2.9 4.9 %collective-permute-start.1 = (f32[4,16,256]{2,1,0:T(8,128)S(1)}, f32[4,16,256]{2,1,0:T(8,128)S(1)}, u32[]{:S(2)}, u32[]{:S(2)}) collective-permute-start(f32[4,16,256]{2,1,0:T(8,128)S(1)} %get-tuple-element.32), channel_id=1, source_target_pairs={{0,16},{1,17},{2,18},{3,19},{4,20},{5,21},{6,22},{7,23},{8,24},{9,... | collective-permute-start | bytes 196616 | tf_op jit(solution)/shard_map/ppermute | solution.py:15
  7.8 0.7 fusion.163
  8.5 0.7 compare_and_fusion
  9.8 0.8 copy.21
  10.6 10.4 %all_gather.7 = bf16[1,4,512]{1,0,2:T(2,128)(2,1)S(1)} all-gather(bf16[1,4,64]{1,0,2:T(2,128)(2,1)S(1)} %copy.21), channel_id=1, replica_groups=mesh['gx'=2,'gy'=4,'shot'=4] {'gx','gy'}, dimensions={2}, use_global_device_ids=true | all-gather | bytes 4608 | tf_op jit(solution)/shard_map/all_gather | solution.py:60
  22.2 1.9 %convolution_bitcast_fusion = f32[4,512,256]{1,2,0:T(8,128)S(1)} fusion(f32[4,64,256]{2,0,1:T(4,128)S(1)} %convolution_bitcast_fusion.1, f32[64]{0:T(128)S(1)} %compare_convert_fusion, s32[64]{0:T(128)S(1)} %bitcast.62), kind=kOutput, calls=%fused_computation.3 | convolution fusion | flops 402718720 | bytes 2359808 | tf_op jit(solution)/shard_map/sc,tsz->tcz/dot_general | solution.py:68
  24.2 2.3 %collective-permute-start.3 = (f32[40,4,256]{2,1,0:T(4,128)S(1)}, f32[40,4,256]{2,1,0:T(4,128)S(1)}, u32[]{:S(2)}, u32[]{:S(2)}) collective-permute-start(f32[40,4,256]{2,1,0:T(4,128)S(1)} %get-tuple-element.23), channel_id=1, source_target_pairs={{0,4},{4,8},{8,12},{1,5},{5,9},{9,13},{2,6},{6,10},{10,14},{3,7},{... | collective-permute-start | bytes 491528 | tf_op jit(solution)/shard_map/ppermute | solution.py:15
  26.5 1.3 collective-permute-start.2
  27.8 1.2 fusion.167
  29.8 0.8 select_maximum_fusion.12
  30.7 0.9 copy-done.3
  31.7 2.0 %fusion.93 = f32[32,16,256]{2,1,0:T(8,128)S(1)} fusion(f32[32,16,256]{2,1,0:T(8,128)S(1)} %bitcast.57, f32[32,16,256]{2,1,0:T(8,128)S(1)} %copy-done.3, f32[32,16,256]{2,1,0:T(8,128)S(1)} %bitcast.54, f32[4,16,256]{2,1,0:T(8,128)S(1)} %collective-permute-done.1, f32[4,16,256]{2,1,0:T(8,128)S(1)} %collective-permute-done, ...), kind=kLoop, calls=%fused_computation.170 | loop fusion | flops 6553600 | bytes 11141120 | tf_op jit(solution)/shard_map/add | solution.py:75
  33.8 1.4 collective-permute-start.4
  35.2 4.5 %collective-permute-start.5 = (f32[4,16,256]{2,1,0:T(8,128)S(1)}, f32[4,16,256]{2,1,0:T(8,128)S(1)}, u32[]{:S(2)}, u32[]{:S(2)}) collective-permute-start(f32[4,16,256]{2,1,0:T(8,128)S(1)} %get-tuple-element.30), channel_id=1, source_target_pairs={{0,16},{1,17},{2,18},{3,19},{4,20},{5,21},{6,22},{7,23},{8,24},{9,... | collective-permute-start | bytes 196616 | tf_op jit(solution)/shard_map/ppermute | solution.py:15
  40.1 1.6 collective-permute-done.5
  41.6 0.8 pad_maximum_fusion.18
  42.4 4.1 %collective-permute-start.7 = (f32[40,4,256]{2,1,0:T(4,128)}, f32[40,4,256]{2,1,0:T(4,128)S(1)}, u32[]{:S(2)}, u32[]{:S(2)}) collective-permute-start(f32[40,4,256]{2,1,0:T(4,128)} %get-tuple-element.19), channel_id=1, source_target_pairs={{0,4},{4,8},{8,12},{1,5},{5,9},{9,13},{2,6},{6,10},{10,14},{3,7},{... | collective-permute-start | bytes 491528 | tf_op jit(solution)/shard_map/ppermute | solution.py:15
  46.5 1.3 collective-permute-start.6
  48.1 2.6 %collective-permute-done.6 = f32[40,4,256]{2,1,0:T(4,128)} collective-permute-done((f32[40,4,256]{2,1,0:T(4,128)}, f32[40,4,256]{2,1,0:T(4,128)}, u32[]{:S(2)}, u32[]{:S(2)}) %collective-permute-start.6) | collective-permute-done | bytes 163872 | tf_op jit(solution)/shard_map/ppermute | solution.py:18
  50.6 1.7 %select_maximum_fusion.8 = f32[40,24,264]{2,1,0:T(8,128)S(1)} fusion(f32[40,4,256]{2,1,0:T(4,128)} %collective-permute-done.6, f32[40,4,256]{2,1,0:T(4,128)S(1)} %collective-permute-done.7, f32[4,16,256]{2,1,0:T(8,128)S(1)} %collective-permute-done.4, f32[32,16,256]{2,1,0:T(8,128)S(1)} %fusion.93, f32[4,16,256]{2,1,0:T(8,128)S(1)} %collective-permute-done.5), kind=kLoop, calls=%fused_computation.12 | loop fusion | flops 3041280 | bytes 1996800 | tf_op jit(solution)/shard_map/concatenate | solution.py:19
  52.3 1.1 pad_maximum_fusion.1
  53.4 2.0 %fusion.66 = f32[32,16,256]{2,1,0:T(8,128)S(1)} fusion(f32[32,16,256]{2,1,0:T(8,128)S(1)} %bitcast.58, f32[32,16,256]{2,1,0:T(8,128)S(1)} %copy-done.3, f32[32,16,256]{2,1,0:T(8,128)S(1)} %fusion.93, f32[4,16,256]{2,1,0:T(8,128)S(1)} %collective-permute-done.5, f32[4,16,256]{2,1,0:T(8,128)S(1)} %collective-permute-done.4, ...), kind=kLoop, calls=%fused_computation.143 | loop fusion | flops 6553600 | bytes 11141120 | tf_op jit(solution)/shard_map/add | solution.py:75
  55.5 1.4 collective-permute-start.8
  56.9 4.5 %collective-permute-start.9 = (f32[4,16,256]{2,1,0:T(8,128)S(1)}, f32[4,16,256]{2,1,0:T(8,128)S(1)}, u32[]{:S(2)}, u32[]{:S(2)}) collective-permute-start(f32[4,16,256]{2,1,0:T(8,128)S(1)} %get-tuple-element.28), channel_id=1, source_target_pairs={{0,16},{1,17},{2,18},{3,19},{4,20},{5,21},{6,22},{7,23},{8,24},{9,... | collective-permute-start | bytes 196616 | tf_op jit(solution)/shard_map/ppermute | solution.py:15
  61.8 1.6 collective-permute-done.9
  63.3 0.8 pad_maximum_fusion.15
  64.1 4.6 %collective-permute-start.11 = (f32[40,4,256]{2,1,0:T(4,128)}, f32[40,4,256]{2,1,0:T(4,128)S(1)}, u32[]{:S(2)}, u32[]{:S(2)}) collective-permute-start(f32[40,4,256]{2,1,0:T(4,128)} %get-tuple-element.15), channel_id=1, source_target_pairs={{0,4},{4,8},{8,12},{1,5},{5,9},{9,13},{2,6},{6,10},{10,14},{3,7},{... | collective-permute-start | bytes 491528 | tf_op jit(solution)/shard_map/ppermute | solution.py:15
  68.7 1.3 collective-permute-start.10
  70.2 2.6 %collective-permute-done.10 = f32[40,4,256]{2,1,0:T(4,128)} collective-permute-done((f32[40,4,256]{2,1,0:T(4,128)}, f32[40,4,256]{2,1,0:T(4,128)}, u32[]{:S(2)}, u32[]{:S(2)}) %collective-permute-start.10) | collective-permute-done | bytes 163872 | tf_op jit(solution)/shard_map/ppermute | solution.py:18
  72.8 1.7 %select_maximum_fusion.4 = f32[40,24,264]{2,1,0:T(8,128)S(1)} fusion(f32[40,4,256]{2,1,0:T(4,128)} %collective-permute-done.10, f32[40,4,256]{2,1,0:T(4,128)S(1)} %collective-permute-done.11, f32[4,16,256]{2,1,0:T(8,128)S(1)} %collective-permute-done.8, f32[32,16,256]{2,1,0:T(8,128)S(1)} %fusion.66, f32[4,16,256]{2,1,0:T(8,128)S(1)} %collective-permute-done.9), kind=kLoop, calls=%fused_computation.8 | loop fusion | flops 3041280 | bytes 1996800 | tf_op jit(solution)/shard_map/concatenate | solution.py:19
  74.5 1.1 pad_maximum_fusion.2
  75.6 2.0 %fusion.39 = f32[32,16,256]{2,1,0:T(8,128)S(1)} fusion(f32[32,16,256]{2,1,0:T(8,128)S(1)} %bitcast.59, f32[32,16,256]{2,1,0:T(8,128)S(1)} %copy-done.3, f32[32,16,256]{2,1,0:T(8,128)S(1)} %fusion.66, f32[4,16,256]{2,1,0:T(8,128)S(1)} %collective-permute-done.9, f32[4,16,256]{2,1,0:T(8,128)S(1)} %collective-permute-done.8, ...), kind=kLoop, calls=%fused_computation.116 | loop fusion | flops 6553600 | bytes 11141120 | tf_op jit(solution)/shard_map/add | solution.py:75
  77.7 4.4 %collective-permute-start.13 = (f32[4,16,256]{2,1,0:T(8,128)S(1)}, f32[4,16,256]{2,1,0:T(8,128)S(1)}, u32[]{:S(2)}, u32[]{:S(2)}) collective-permute-start(f32[4,16,256]{2,1,0:T(8,128)S(1)} %get-tuple-element.25), channel_id=1, source_target_pairs={{0,16},{1,17},{2,18},{3,19},{4,20},{5,21},{6,22},{7,23},{8,24},{9,... | collective-permute-start | bytes 196616 | tf_op jit(solution)/shard_map/ppermute | solution.py:15
  82.1 1.3 collective-permute-start.12
  84.0 4.3 %collective-permute-done.12 = f32[4,16,256]{2,1,0:T(8,128)S(1)} collective-permute-done((f32[4,16,256]{2,1,0:T(8,128)S(1)}, f32[4,16,256]{2,1,0:T(8,128)S(1)}, u32[]{:S(2)}, u32[]{:S(2)}) %collective-permute-start.12) | collective-permute-done | bytes 65568 | tf_op jit(solution)/shard_map/ppermute | solution.py:18
  88.2 0.8 pad_maximum_fusion.12
  89.0 4.3 %collective-permute-start.15 = (f32[40,4,256]{2,1,0:T(4,128)}, f32[40,4,256]{2,1,0:T(4,128)S(1)}, u32[]{:S(2)}, u32[]{:S(2)}) collective-permute-start(f32[40,4,256]{2,1,0:T(4,128)} %get-tuple-element.11), channel_id=1, source_target_pairs={{0,4},{4,8},{8,12},{1,5},{5,9},{9,13},{2,6},{6,10},{10,14},{3,7},{... | collective-permute-start | bytes 491528 | tf_op jit(solution)/shard_map/ppermute | solution.py:15
  93.3 1.5 collective-permute-start.14
  94.8 1.0 copy.28
  95.8 1.9 %collective-permute-done.14 = f32[40,4,256]{2,1,0:T(4,128)} collective-permute-done((f32[40,4,256]{2,1,0:T(4,128)}, f32[40,4,256]{2,1,0:T(4,128)}, u32[]{:S(2)}, u32[]{:S(2)}) %collective-permute-start.14) | collective-permute-done | bytes 163872 | tf_op jit(solution)/shard_map/ppermute | solution.py:18
  97.7 1.7 %select_maximum_fusion = f32[40,24,264]{2,1,0:T(8,128)S(1)} fusion(f32[40,4,256]{2,1,0:T(4,128)} %collective-permute-done.14, f32[40,4,256]{2,1,0:T(4,128)S(1)} %collective-permute-done.15, f32[4,16,256]{2,1,0:T(8,128)S(1)} %collective-permute-done.12, f32[32,16,256]{2,1,0:T(8,128)S(1)} %fusion.39, f32[4,16,256]{2,1,0:T(8,128)S(1)} %collective-permute-done.13), kind=kLoop, calls=%fused_computation.4 | loop fusion | flops 3041280 | bytes 1996800 | tf_op jit(solution)/shard_map/concatenate | solution.py:19
  99.4 1.2 pad_maximum_fusion.3
  100.9 2.9 %fusion.149 = (f32[32,16,256]{2,1,0:T(8,128)S(1)}, f32[32,16,256]{2,1,0:T(8,128)}) fusion(f32[32,16,256]{2,1,0:T(8,128)S(1)} %fusion.39, f32[32,16,256]{2,1,0:T(8,128)S(1)} %fusion.66, f32[32,16,256]{2,1,0:T(8,128)S(1)} %fusion.93, bf16[1,4,32,16,256]{4,3,2,1,0:T(8,128)(2,1)S(1)} %copy-done.8, f32[32,16,256]{2,1,0:T(8,128)S(1)} %bitcast.56, ...), kind=kLoop, calls=%fused_computation.267 | loop fusion | flops 7995392 | bytes 13238272 | tf_op jit(solution)/shard_map/add | solution.py:80
  103.7 34.8 %reshape.77 = f32[16,2,8,2,128,2]{5,4,3,2,1,0:T(8,128)} reshape(f32[32,16,256]{2,1,0:T(8,128)S(1)} %get-tuple-element.3) | data formatting | bytes 1048576 | tf_op jit(solution)/shard_map/reshape | solution.py:50
  138.6 12.2 %reduce_sum.18 = f32[16,8,128]{2,1,0:T(8,128)S(1)} reduce(f32[16,2,8,2,128,2]{5,4,3,2,1,0:T(8,128)} %reshape.77, f32[]{:T(128)} %constant.9.clone.1), dimensions={1,3,5}, to_apply=%region_0.1 | reduce | flops 114688 | bytes 589828 | tf_op jit(solution)/shard_map/reduce_sum | solution.py:50
  150.8 14.8 %all-gather = f32[64,8,128]{2,1,0:T(8,128)S(1)} all-gather(f32[16,8,128]{2,1,0:T(8,128)S(1)} %broadcast_multiply_fusion), channel_id=2, replica_groups=mesh['gx'=2,'gy'=4,'shot'=4] {'shot'}, dimensions={0}, use_global_device_ids=true | all-gather | bytes 327680 | tf_op jit(solution)/shard_map/all_gather | solution.py:83
  (48 shorter events, 4.9 us)
Async XLA Ops:
  0.6 21.3 %copy-start = (bf16[1,1,64,16,256]{4,3,2,1,0:T(8,128)(2,1)S(1)}, bf16[1,1,64,16,256]{4,3,2,1,0:T(8,128)(2,1)}, u32[]{:S(2)}) copy-start(bf16[1,1,64,16,256]{4,3,2,1,0:T(8,128)(2,1)} %param.14) | copy-start | bytes 1572868
  0.6 21.6 %copy-start.10 = (s32[1,1,64]{2,1,0:T(1,128)S(1)}, s32[1,1,64]{2,1,0:T(1,128)}, u32[]{:S(2)}) copy-start(s32[1,1,64]{2,1,0:T(1,128)} %param.16) | copy-start | bytes 772
  1.6 22.5 %collective-permute-start = (f32[4,16,256]{2,1,0:T(8,128)S(1)}, f32[4,16,256]{2,1,0:T(8,128)S(1)}, u32[]{:S(2)}, u32[]{:S(2)}) collective-permute-start(f32[4,16,256]{2,1,0:T(8,128)S(1)} %get-tuple-element.31), channel_id=1, source_target_pairs={{16,0},{17,1},{18,2},{19,3},{20,4},{21,5},{22,6},{23,7},{24,8},{25... | collective-permute-start | bytes 196616 | tf_op jit(solution)/shard_map/ppermute | solution.py:18
  2.9 21.2 %collective-permute-start.1 = (f32[4,16,256]{2,1,0:T(8,128)S(1)}, f32[4,16,256]{2,1,0:T(8,128)S(1)}, u32[]{:S(2)}, u32[]{:S(2)}) collective-permute-start(f32[4,16,256]{2,1,0:T(8,128)S(1)} %get-tuple-element.32), channel_id=1, source_target_pairs={{0,16},{1,17},{2,18},{3,19},{4,20},{5,21},{6,22},{7,23},{8,24},{9,... | collective-permute-start | bytes 196616 | tf_op jit(solution)/shard_map/ppermute | solution.py:15
  21.9 2.2 %copy-start.1 = (f32[1,32,16,256]{3,2,1,0:T(8,128)S(1)}, f32[1,32,16,256]{3,2,1,0:T(8,128)}, u32[]{:S(2)}) copy-start(f32[1,32,16,256]{3,2,1,0:T(8,128)} %param.10) | copy-start | bytes 1572868
  24.2 4.9 %collective-permute-start.3 = (f32[40,4,256]{2,1,0:T(4,128)S(1)}, f32[40,4,256]{2,1,0:T(4,128)S(1)}, u32[]{:S(2)}, u32[]{:S(2)}) collective-permute-start(f32[40,4,256]{2,1,0:T(4,128)S(1)} %get-tuple-element.23), channel_id=1, source_target_pairs={{0,4},{4,8},{8,12},{1,5},{5,9},{9,13},{2,6},{6,10},{10,14},{3,7},{... | collective-permute-start | bytes 491528 | tf_op jit(solution)/shard_map/ppermute | solution.py:15
  26.5 3.3 %collective-permute-start.2 = (f32[40,4,256]{2,1,0:T(4,128)S(1)}, f32[40,4,256]{2,1,0:T(4,128)S(1)}, u32[]{:S(2)}, u32[]{:S(2)}) collective-permute-start(f32[40,4,256]{2,1,0:T(4,128)S(1)} %get-tuple-element.24), channel_id=1, source_target_pairs={{4,0},{8,4},{12,8},{5,1},{9,5},{13,9},{6,2},{10,6},{14,10},{7,3},{... | collective-permute-start | bytes 491528 | tf_op jit(solution)/shard_map/ppermute | solution.py:18
  30.5 1.0 copy-start.3
  30.5 1.2 copy-start.9
  33.7 14.1 %copy-start.7 = (f32[1,512,256]{1,2,0:T(8,128)S(1)}, f32[1,512,256]{1,2,0:T(8,128)}, u32[]{:S(2)}) copy-start(f32[1,512,256]{1,2,0:T(8,128)} %get-tuple-element.7) | copy-start | bytes 1572868
  33.8 6.3 %collective-permute-start.4 = (f32[4,16,256]{2,1,0:T(8,128)S(1)}, f32[4,16,256]{2,1,0:T(8,128)S(1)}, u32[]{:S(2)}, u32[]{:S(2)}) collective-permute-start(f32[4,16,256]{2,1,0:T(8,128)S(1)} %get-tuple-element.29), channel_id=1, source_target_pairs={{16,0},{17,1},{18,2},{19,3},{20,4},{21,5},{22,6},{23,7},{24,8},{25... | collective-permute-start | bytes 196616 | tf_op jit(solution)/shard_map/ppermute | solution.py:18
  35.2 6.4 %collective-permute-start.5 = (f32[4,16,256]{2,1,0:T(8,128)S(1)}, f32[4,16,256]{2,1,0:T(8,128)S(1)}, u32[]{:S(2)}, u32[]{:S(2)}) collective-permute-start(f32[4,16,256]{2,1,0:T(8,128)S(1)} %get-tuple-element.30), channel_id=1, source_target_pairs={{0,16},{1,17},{2,18},{3,19},{4,20},{5,21},{6,22},{7,23},{8,24},{9,... | collective-permute-start | bytes 196616 | tf_op jit(solution)/shard_map/ppermute | solution.py:15
  42.4 5.6 %collective-permute-start.7 = (f32[40,4,256]{2,1,0:T(4,128)}, f32[40,4,256]{2,1,0:T(4,128)S(1)}, u32[]{:S(2)}, u32[]{:S(2)}) collective-permute-start(f32[40,4,256]{2,1,0:T(4,128)} %get-tuple-element.19), channel_id=1, source_target_pairs={{0,4},{4,8},{8,12},{1,5},{5,9},{9,13},{2,6},{6,10},{10,14},{3,7},{... | collective-permute-start | bytes 491528 | tf_op jit(solution)/shard_map/ppermute | solution.py:15
  46.5 4.1 %collective-permute-start.6 = (f32[40,4,256]{2,1,0:T(4,128)}, f32[40,4,256]{2,1,0:T(4,128)}, u32[]{:S(2)}, u32[]{:S(2)}) collective-permute-start(f32[40,4,256]{2,1,0:T(4,128)} %get-tuple-element.20), channel_id=1, source_target_pairs={{4,0},{8,4},{12,8},{5,1},{9,5},{13,9},{6,2},{10,6},{14,10},{7,3},{... | collective-permute-start | bytes 491528 | tf_op jit(solution)/shard_map/ppermute | solution.py:18
  55.4 14.6 %copy-start.6 = (f32[1,512,256]{1,2,0:T(8,128)S(1)}, f32[1,512,256]{1,2,0:T(8,128)}, u32[]{:S(2)}) copy-start(f32[1,512,256]{1,2,0:T(8,128)} %get-tuple-element.6) | copy-start | bytes 1572868
  55.5 6.3 %collective-permute-start.8 = (f32[4,16,256]{2,1,0:T(8,128)S(1)}, f32[4,16,256]{2,1,0:T(8,128)S(1)}, u32[]{:S(2)}, u32[]{:S(2)}) collective-permute-start(f32[4,16,256]{2,1,0:T(8,128)S(1)} %get-tuple-element.27), channel_id=1, source_target_pairs={{16,0},{17,1},{18,2},{19,3},{20,4},{21,5},{22,6},{23,7},{24,8},{25... | collective-permute-start | bytes 196616 | tf_op jit(solution)/shard_map/ppermute | solution.py:18
  56.9 6.4 %collective-permute-start.9 = (f32[4,16,256]{2,1,0:T(8,128)S(1)}, f32[4,16,256]{2,1,0:T(8,128)S(1)}, u32[]{:S(2)}, u32[]{:S(2)}) collective-permute-start(f32[4,16,256]{2,1,0:T(8,128)S(1)} %get-tuple-element.28), channel_id=1, source_target_pairs={{0,16},{1,17},{2,18},{3,19},{4,20},{5,21},{6,22},{7,23},{8,24},{9,... | collective-permute-start | bytes 196616 | tf_op jit(solution)/shard_map/ppermute | solution.py:15
  64.1 6.1 %collective-permute-start.11 = (f32[40,4,256]{2,1,0:T(4,128)}, f32[40,4,256]{2,1,0:T(4,128)S(1)}, u32[]{:S(2)}, u32[]{:S(2)}) collective-permute-start(f32[40,4,256]{2,1,0:T(4,128)} %get-tuple-element.15), channel_id=1, source_target_pairs={{0,4},{4,8},{8,12},{1,5},{5,9},{9,13},{2,6},{6,10},{10,14},{3,7},{... | collective-permute-start | bytes 491528 | tf_op jit(solution)/shard_map/ppermute | solution.py:15
  68.7 4.1 %collective-permute-start.10 = (f32[40,4,256]{2,1,0:T(4,128)}, f32[40,4,256]{2,1,0:T(4,128)}, u32[]{:S(2)}, u32[]{:S(2)}) collective-permute-start(f32[40,4,256]{2,1,0:T(4,128)} %get-tuple-element.16), channel_id=1, source_target_pairs={{4,0},{8,4},{12,8},{5,1},{9,5},{13,9},{6,2},{10,6},{14,10},{7,3},{... | collective-permute-start | bytes 491528 | tf_op jit(solution)/shard_map/ppermute | solution.py:18
  77.6 23.0 %copy-start.2 = (f32[32,16,256]{2,1,0:T(8,128)}, f32[32,16,256]{2,1,0:T(8,128)S(1)}, u32[]{:S(2)}) copy-start(f32[32,16,256]{2,1,0:T(8,128)S(1)} %fusion.39) | copy-start | bytes 1572868
  77.6 17.2 %copy-start.5 = (f32[1,512,256]{1,2,0:T(8,128)S(1)}, f32[1,512,256]{1,2,0:T(8,128)}, u32[]{:S(2)}) copy-start(f32[1,512,256]{1,2,0:T(8,128)} %get-tuple-element.5) | copy-start | bytes 1572868
  77.7 6.3 %collective-permute-start.13 = (f32[4,16,256]{2,1,0:T(8,128)S(1)}, f32[4,16,256]{2,1,0:T(8,128)S(1)}, u32[]{:S(2)}, u32[]{:S(2)}) collective-permute-start(f32[4,16,256]{2,1,0:T(8,128)S(1)} %get-tuple-element.25), channel_id=1, source_target_pairs={{0,16},{1,17},{2,18},{3,19},{4,20},{5,21},{6,22},{7,23},{8,24},{9,... | collective-permute-start | bytes 196616 | tf_op jit(solution)/shard_map/ppermute | solution.py:15
  82.1 6.2 %collective-permute-start.12 = (f32[4,16,256]{2,1,0:T(8,128)S(1)}, f32[4,16,256]{2,1,0:T(8,128)S(1)}, u32[]{:S(2)}, u32[]{:S(2)}) collective-permute-start(f32[4,16,256]{2,1,0:T(8,128)S(1)} %get-tuple-element.26), channel_id=1, source_target_pairs={{16,0},{17,1},{18,2},{19,3},{20,4},{21,5},{22,6},{23,7},{24,8},{25... | collective-permute-start | bytes 196616 | tf_op jit(solution)/shard_map/ppermute | solution.py:18
  89.0 6.8 %collective-permute-start.15 = (f32[40,4,256]{2,1,0:T(4,128)}, f32[40,4,256]{2,1,0:T(4,128)S(1)}, u32[]{:S(2)}, u32[]{:S(2)}) collective-permute-start(f32[40,4,256]{2,1,0:T(4,128)} %get-tuple-element.11), channel_id=1, source_target_pairs={{0,4},{4,8},{8,12},{1,5},{5,9},{9,13},{2,6},{6,10},{10,14},{3,7},{... | collective-permute-start | bytes 491528 | tf_op jit(solution)/shard_map/ppermute | solution.py:15
  93.3 4.4 %collective-permute-start.14 = (f32[40,4,256]{2,1,0:T(4,128)}, f32[40,4,256]{2,1,0:T(4,128)}, u32[]{:S(2)}, u32[]{:S(2)}) collective-permute-start(f32[40,4,256]{2,1,0:T(4,128)} %get-tuple-element.12), channel_id=1, source_target_pairs={{4,0},{8,4},{12,8},{5,1},{9,5},{13,9},{6,2},{10,6},{14,10},{7,3},{... | collective-permute-start | bytes 491528 | tf_op jit(solution)/shard_map/ppermute | solution.py:18
  99.4 1.2 copy-start.4
  99.4 1.5 copy-start.8
